TPU v7x, 32 devices: a whole 2x2x4 slice. The times are simulated.
32 devices in a mesh: dp: 2 (over core), row: 4 (over y, x), col: 4 (over z).
Axes of the slice: x: 2, y: 2, z: 4, core: 2. Of those that a mesh axis runs over, the one named last changes fastest.
Arguments:
- tokens: bfloat16 [768, 8192], P('row', ('dp', 'col')), may hold values from -6 to 6
- prefix: int32 [8], P(('dp', 'row')), may hold values from 102 to 512, as said below
- ln1_gain: float32 [768], replicated, may hold values from 0.5 to 1.5
- ln1_bias: float32 [768], replicated, may hold values from -3 to 3
- w_qkv: bfloat16 [3, 768, 768], P(None, 'row', 'col'), may hold values from -0.21875 to 0.21875
- qv_bias: float32 [2, 768], replicated, may hold values from -3 to 3
- w_out: bfloat16 [768, 768], P('col', 'row'), may hold values from -0.875 to 0.875
- out_bias: float32 [768], replicated, may hold values from -3 to 3
- ln2_gain: float32 [768], replicated, may hold values from 0.5 to 1.5
- ln2_bias: float32 [768], replicated, may hold values from -3 to 3
- w_fc: bfloat16 [768, 3072], P('row', 'col'), may hold values from -0.21875 to 0.21875
- fc_bias: float32 [3072], replicated, may hold values from -3 to 3
- w_proj: bfloat16 [768, 3072], P('row', 'col'), may hold values from -0.109375 to 0.109375
- proj_bias: float32 [768], replicated, may hold values from -3 to 3
- cotangent: bfloat16 [768, 8192], P('row', ('dp', 'col')), may hold values from -6 to 6
Outputs:
- output: bfloat16 [768, 8192], P('row', ('dp', 'col'))
- input_grad: float32 [768, 8192], P('row', ('dp', 'col'))
- ln1_gain_grad: float32 [768], replicated
- ln1_bias_grad: float32 [768], replicated
- w_qkv_grad: float32 [3, 768, 768], P(None, 'row', 'col')
- qv_bias_grad: float32 [2, 768], replicated
- w_out_grad: float32 [768, 768], P('col', 'row')
- out_bias_grad: float32 [768], replicated
- ln2_gain_grad: float32 [768], replicated
- ln2_bias_grad: float32 [768], replicated
- w_fc_grad: float32 [768, 3072], P('row', 'col')
- fc_bias_grad: float32 [3072], replicated
- w_proj_grad: float32 [768, 3072], P('row', 'col')
- proj_bias_grad: float32 [768], replicated
Inputs may be any that keep to these rules, and one draw needn't show every extreme that they name: `prefix`: in every draw some sequence has exactly 102 and some other exactly 512.
All inputs are finite; a program needn't handle non-finite values.
Results may differ from a plain program's by a relative error of at most 0.012.
Values may be sent and summed in bfloat16 or wider, within the bound.
A program may use at most 256 MiB of HBM per device.

v0:
```python
import jax
import jax.numpy as jnp
from jax import lax
from jax.sharding import PartitionSpec as P

D = 768
FF = 3072
HEAD_DIM = 64
LEN = 1024
epsilon = 1e-05
masked_score = -1e30


def feature_totals(values):
    return lax.psum(values, "row")


def column_rows(values):
    return lax.all_gather(values, "col", axis=0, tiled=True)


def row_rows(values):
    return lax.all_gather(values, "row", axis=0, tiled=True)


def summed_over_row(term_fn, row_count):
    return lax.psum_scatter(
        term_fn(jnp.int32(0), row_count * lax.axis_size("row")),
        "row",
        scatter_dimension=0,
        tiled=True,
    )


def summed_over_col(term_fn, row_count):
    return lax.psum_scatter(
        term_fn(jnp.int32(0), row_count * lax.axis_size("col")),
        "col",
        scatter_dimension=0,
        tiled=True,
    )


def take_portion(complete, position, portion_size, along):
    return lax.dynamic_slice_in_dim(complete, position * portion_size, portion_size, along)


def place_portion(portion, position, full_size, along):
    zeroed_shape = portion.shape[:along] + (full_size,) + portion.shape[along + 1 :]
    zeroed = jnp.zeros(zeroed_shape, jnp.float32)
    return lax.dynamic_update_slice_in_dim(zeroed, portion, position * portion.shape[along], along)


def gelu_tanh(values):
    return jax.nn.gelu(values, approximate=True)


def norm_forward(values, norm_gain, norm_offset, totals_fn):
    plain_sum, square_sum = totals_fn((jnp.sum(values, axis=1), jnp.sum(values * values, axis=1)))
    center = (plain_sum / D)[:, None]
    inverse = lax.rsqrt(square_sum[:, None] / D - center * center + epsilon)
    unit_rows = (values - center) * inverse
    return (unit_rows * norm_gain + norm_offset, unit_rows, inverse)


def norm_backward(grad_rows, unit_rows, inverse, norm_gain, totals_fn):
    scaled = grad_rows * norm_gain
    plain_sum, cross_sum = totals_fn((jnp.sum(scaled, axis=1), jnp.sum(scaled * unit_rows, axis=1)))
    return inverse * (scaled - (plain_sum / D)[:, None] - unit_rows * (cross_sum / D)[:, None])


def split_heads(flat_rows):
    return flat_rows.reshape(LEN, flat_rows.shape[1] // HEAD_DIM, HEAD_DIM)


def scores_of(queries, keys_block, limit_value):
    raw_scores = jnp.einsum("qhe,khe->hqk", queries, keys_block, preferred_element_type=jnp.float32)
    raw_scores = raw_scores * HEAD_DIM ** (-0.5)
    places = jnp.arange(LEN, dtype=jnp.int32)
    visible = (places[None, :] <= places[:, None]) | (places[None, :] < limit_value)
    return jnp.where(visible[None], raw_scores, masked_score)


def attend_forward(packed):
    block_rows, limit_value = packed
    queries = split_heads(block_rows[:, 0])
    keys_block = split_heads(block_rows[:, 1])
    values_block = split_heads(block_rows[:, 2])
    scores = scores_of(queries, keys_block, limit_value)
    largest = jnp.max(scores, axis=-1, keepdims=True)
    weights = jnp.exp(scores - largest)
    row_totals = jnp.sum(weights, axis=-1, keepdims=True)
    probs = (weights / row_totals).astype(jnp.bfloat16)
    mixed = jnp.einsum("hqk,khe->qhe", probs, values_block, preferred_element_type=jnp.float32)
    return (mixed.reshape(LEN, -1).astype(jnp.bfloat16), (largest + jnp.log(row_totals))[..., 0])


def attend_backward(packed):
    block_rows, limit_value, log_total, out_grad = packed
    queries = split_heads(block_rows[:, 0])
    keys_block = split_heads(block_rows[:, 1])
    values_block = split_heads(block_rows[:, 2])
    scores = scores_of(queries, keys_block, limit_value)
    probs = jnp.exp(scores - log_total[..., None])
    probs_low = probs.astype(jnp.bfloat16)
    grad_heads = split_heads(out_grad)
    weight_grad = jnp.einsum(
        "qhe,khe->hqk", grad_heads, values_block, preferred_element_type=jnp.float32
    )
    row_inner = jnp.sum(probs * weight_grad, axis=-1, keepdims=True)
    score_grad = (probs * (weight_grad - row_inner)).astype(jnp.bfloat16)
    query_grad = jnp.einsum(
        "hqk,khe->qhe", score_grad, keys_block, preferred_element_type=jnp.float32
    )
    key_grad = jnp.einsum("hqk,qhe->khe", score_grad, queries, preferred_element_type=jnp.float32)
    value_grad = jnp.einsum(
        "hqk,qhe->khe", probs_low, grad_heads, preferred_element_type=jnp.float32
    )
    score_factor = HEAD_DIM ** (-0.5)
    stacked = jnp.stack(
        [
            (query_grad * score_factor).reshape(LEN, -1),
            (key_grad * score_factor).reshape(LEN, -1),
            value_grad.reshape(LEN, -1),
        ],
        axis=1,
    )
    return stacked.astype(jnp.bfloat16)


def on_device(
    tokens,
    prefix,
    ln1_gain,
    ln1_bias,
    w_qkv,
    qv_bias,
    w_out,
    out_bias,
    ln2_gain,
    ln2_bias,
    w_fc,
    fc_bias,
    w_proj,
    proj_bias,
    cotangent,
):
    row_place = lax.axis_index("row")
    col_place = lax.axis_index("col")
    row_devices = lax.axis_size("row")
    col_devices = lax.axis_size("col")
    width_row, local_rows = tokens.shape
    width_col = w_qkv.shape[2]
    hidden_col = w_fc.shape[1]
    seq_rows = local_rows * col_devices // row_devices
    seq_count = seq_rows // LEN
    residual = tokens.T.astype(jnp.float32)
    cotangent_local = cotangent.T
    first_gain = take_portion(ln1_gain, row_place, width_row, 0)
    first_normed, first_unit, first_inverse = norm_forward(
        residual, first_gain, take_portion(ln1_bias, row_place, width_row, 0), feature_totals
    )
    first_gathered = column_rows(first_normed.astype(jnp.bfloat16))

    def qkv_term(first_row, row_count):
        return jnp.einsum("td,sde->tse", first_gathered, w_qkv, preferred_element_type=jnp.float32)

    bias_col = take_portion(qv_bias, col_place, width_col, 1)
    bias_rows = jnp.stack([bias_col[0], jnp.zeros_like(bias_col[0]), bias_col[1]])
    qkv_sum = summed_over_row(qkv_term, seq_rows)
    qkv = (qkv_sum + bias_rows).astype(jnp.bfloat16)
    blocks = qkv.reshape(seq_count, LEN, 3, width_col)
    attn_blocks, log_totals = lax.map(attend_forward, (blocks, prefix))
    attn = attn_blocks.reshape(seq_rows, width_col)
    attn_gathered = row_rows(attn)

    def out_term(first_row, row_count):
        return jnp.dot(attn_gathered, w_out, preferred_element_type=jnp.float32)

    middle = (
        residual
        + summed_over_col(out_term, local_rows)
        + take_portion(out_bias, row_place, width_row, 0)
    )
    grad_output = cotangent_local.astype(jnp.float32)
    second_gain = take_portion(ln2_gain, row_place, width_row, 0)
    second_normed, second_unit, second_inverse = norm_forward(
        middle, second_gain, take_portion(ln2_bias, row_place, width_row, 0), feature_totals
    )
    second_gathered = column_rows(second_normed.astype(jnp.bfloat16))

    def up_term(first_row, row_count):
        return jnp.dot(second_gathered, w_fc, preferred_element_type=jnp.float32)

    hidden = summed_over_row(up_term, seq_rows) + take_portion(fc_bias, col_place, hidden_col, 0)
    active, gelu_pull = jax.vjp(gelu_tanh, hidden)
    active_gathered = row_rows(active.astype(jnp.bfloat16))

    def down_term(first_row, row_count):
        return jnp.einsum("tf,df->td", active_gathered, w_proj, preferred_element_type=jnp.float32)

    final_rows = (
        middle
        + summed_over_col(down_term, local_rows)
        + take_portion(proj_bias, row_place, width_row, 0)
    )
    output = final_rows.astype(jnp.bfloat16)
    grad_gathered = column_rows(cotangent_local)
    w_proj_grad = jnp.einsum(
        "tf,td->df", active_gathered, grad_gathered, preferred_element_type=jnp.float32
    )

    def active_term(first_row, row_count):
        return jnp.einsum("td,df->tf", grad_gathered, w_proj, preferred_element_type=jnp.float32)

    hidden_grad = gelu_pull(summed_over_row(active_term, seq_rows))[0].astype(jnp.bfloat16)
    hidden_gathered = row_rows(hidden_grad)
    w_fc_grad = jnp.einsum(
        "td,tf->df", second_gathered, hidden_gathered, preferred_element_type=jnp.float32
    )

    def second_term(first_row, row_count):
        return jnp.einsum("tf,df->td", hidden_gathered, w_fc, preferred_element_type=jnp.float32)

    second_grad = summed_over_col(second_term, local_rows)
    middle_grad = grad_output + norm_backward(
        second_grad, second_unit, second_inverse, second_gain, feature_totals
    )
    ln2_gain_part = place_portion(jnp.sum(second_grad * second_unit, axis=0), row_place, D, 0)
    ln2_bias_part = place_portion(jnp.sum(second_grad, axis=0), row_place, D, 0)
    fc_bias_part = place_portion(jnp.sum(hidden_grad.astype(jnp.float32), axis=0), col_place, FF, 0)
    proj_bias_part = place_portion(jnp.sum(grad_output, axis=0), row_place, D, 0)
    branch_grad = middle_grad.astype(jnp.bfloat16)
    branch_gathered = column_rows(branch_grad)
    w_out_grad = jnp.einsum(
        "te,td->ed", attn_gathered, branch_gathered, preferred_element_type=jnp.float32
    )

    def attn_term(first_row, row_count):
        return jnp.einsum("td,ed->te", branch_gathered, w_out, preferred_element_type=jnp.float32)

    attn_grad = summed_over_row(attn_term, seq_rows).astype(jnp.bfloat16)
    qkv_grad = lax.map(
        attend_backward, (blocks, prefix, log_totals, attn_grad.reshape(seq_count, LEN, width_col))
    )
    qkv_grad = qkv_grad.reshape(seq_rows, 3, width_col)
    qkv_gathered = row_rows(qkv_grad)
    w_qkv_grad = jnp.einsum(
        "td,tse->sde", first_gathered, qkv_gathered, preferred_element_type=jnp.float32
    )

    def first_term(first_row, row_count):
        return jnp.einsum("tse,sde->td", qkv_gathered, w_qkv, preferred_element_type=jnp.float32)

    first_grad = summed_over_col(first_term, local_rows)
    input_grad = middle_grad + norm_backward(
        first_grad, first_unit, first_inverse, first_gain, feature_totals
    )
    qkv_totals = jnp.sum(qkv_grad.astype(jnp.float32), axis=0)
    qv_part = place_portion(jnp.stack([qkv_totals[0], qkv_totals[2]]), col_place, D, 1)
    out_bias_part = place_portion(jnp.sum(branch_grad.astype(jnp.float32), axis=0), row_place, D, 0)
    ln1_gain_part = place_portion(jnp.sum(first_grad * first_unit, axis=0), row_place, D, 0)
    ln1_bias_part = place_portion(jnp.sum(first_grad, axis=0), row_place, D, 0)
    vectors = lax.psum(
        (
            ln1_gain_part,
            ln1_bias_part,
            qv_part,
            out_bias_part,
            ln2_gain_part,
            ln2_bias_part,
            fc_bias_part,
            proj_bias_part,
        ),
        ("dp", "row", "col"),
    )
    matrices = (
        lax.psum(w_qkv_grad.astype(jnp.bfloat16), "dp").astype(jnp.float32),
        lax.psum(w_out_grad.astype(jnp.bfloat16), "dp").astype(jnp.float32),
        lax.psum(w_fc_grad.astype(jnp.bfloat16), "dp").astype(jnp.float32),
        lax.psum(w_proj_grad.astype(jnp.bfloat16), "dp").astype(jnp.float32),
    )
    return (
        output.T,
        input_grad.T,
        vectors[0],
        vectors[1],
        matrices[0],
        vectors[2],
        matrices[1],
        vectors[3],
        vectors[4],
        vectors[5],
        matrices[2],
        vectors[6],
        matrices[3],
        vectors[7],
    )


def solution(mesh):
    placed = (
        P("row", ("dp", "col")),
        P(("dp", "row")),
        P(),
        P(),
        P(None, "row", "col"),
        P(),
        P("col", "row"),
        P(),
        P(),
        P(),
        P("row", "col"),
        P(),
        P("row", "col"),
        P(),
        P("row", ("dp", "col")),
    )
    return jax.shard_map(
        on_device,
        mesh=mesh,
        in_specs=placed,
        out_specs=(
            P("row", ("dp", "col")),
            P("row", ("dp", "col")),
            P(),
            P(),
            P(None, "row", "col"),
            P(),
            P("col", "row"),
            P(),
            P(),
            P(),
            P("row", "col"),
            P(),
            P("row", "col"),
            P(),
        ),
        check_vma=False,
    )
```

profile of v0, /device:TPU:0, one launch (start us, length us, event | category | flops | bytes accessed | tf_op | source)
XLA Modules:
  0.0 1165.3 jit_solution(17599242956197801233)
XLA Ops:
  7.2 1.1 convert_reduce_fusion.3
  8.3 1.1 fusion.45
  11.0 11.5 all-reduce.4
  22.5 1.9 fusion.38
  24.5 1.1 copy.29
  25.6 35.4 %all-gather.9.cloned.1.call-done = bf16[4096,192]{0,1:T(8,128)(2,1)} async-done(((bf16[1024,192]{0,1:T(8,128)(2,1)}), bf16[4096,192]{0,1:T(8,128)(2,1)}) %all-gather.9.cloned.1.call-update) | async-done | bytes 1572880 | tf_op jit(solution)/shard_map/all_gather | solution.py:19
  61.1 6.4 fusion.61
  69.5 92.0 %reduce-scatter.9.cloned.1.call-done = f32[1024,3,192]{0,2,1:T(8,128)} async-done(((f32[4096,3,192]{0,2,1:T(8,128)}), f32[1024,3,192]{0,2,1:T(8,128)}) %reduce-scatter.9.cloned.1.call-update) | async-done | bytes 2359312 | tf_op jit(solution)/shard_map/reduce_scatter | solution.py:27
  161.5 1.9 add_convert_fusion
  163.5 3.2 fusion.55
  166.8 1.7 fusion
  168.5 2.8 copy-done.2
  171.3 3.0 fusion.21
  174.4 31.1 %all-gather.11.cloned.1.call-done = bf16[4096,192]{0,1:T(8,128)(2,1)} async-done(((bf16[1024,192]{0,1:T(8,128)(2,1)}), bf16[4096,192]{0,1:T(8,128)(2,1)}) %all-gather.11.cloned.1.call-update) | async-done | bytes 1572880 | tf_op jit(solution)/shard_map/all_gather | solution.py:23
  205.5 3.7 fusion.56
  212.1 57.5 %reduce-scatter.11.cloned.1.call-done = f32[1024,192]{0,1:T(8,128)} async-done(((f32[4096,192]{0,1:T(8,128)}), f32[1024,192]{0,1:T(8,128)}) %reduce-scatter.11.cloned.1.call-update) | async-done | bytes 786448 | tf_op jit(solution)/shard_map/reduce_scatter | solution.py:36
  269.6 1.3 fusion.49
  270.9 10.1 all-reduce.3
  281.0 1.0 add_convert_fusion.2
  282.1 26.1 %all-gather.17.cloned.1.call-done = bf16[4096,192]{0,1:T(8,128)(2,1)} async-done(((bf16[1024,192]{0,1:T(8,128)(2,1)}), bf16[4096,192]{0,1:T(8,128)(2,1)}) %all-gather.17.cloned.1.call-update) | async-done | bytes 1572880 | tf_op jit(solution)/shard_map/all_gather | solution.py:19
  308.2 7.7 fusion.59
  316.2 30.0 %all-gather.13.cloned.1.call-done = bf16[4096,192]{0,1:T(8,128)(2,1)} async-done(((bf16[1024,192]{0,1:T(8,128)(2,1)}), bf16[4096,192]{0,1:T(8,128)(2,1)}) %all-gather.13.cloned.1.call-update) | async-done | bytes 1572880 | tf_op jit(solution)/shard_map/all_gather | solution.py:19
  346.2 7.9 fusion.57
  354.9 114.0 %reduce-scatter.17.cloned.1.call-done = f32[1024,768]{1,0:T(8,128)} async-done(((f32[4096,768]{1,0:T(8,128)}), f32[1024,768]{1,0:T(8,128)}) %reduce-scatter.17.cloned.1.call-update) | async-done | bytes 3145744 | tf_op jit(solution)/shard_map/reduce_scatter | solution.py:27
  468.9 123.9 %reduce-scatter.13.cloned.1.call-done = f32[1024,768]{1,0:T(8,128)} async-done(((f32[4096,768]{1,0:T(8,128)}), f32[1024,768]{1,0:T(8,128)}) %reduce-scatter.13.cloned.1.call-update) | async-done | bytes 3145744 | tf_op jit(solution)/shard_map/reduce_scatter | solution.py:27
  592.7 5.6 convert_reduce_fusion
  598.5 70.2 %all-gather.19.cloned.1.call-done = bf16[4096,768]{1,0:T(8,128)(2,1)} async-done(((bf16[1024,768]{1,0:T(8,128)(2,1)}), bf16[4096,768]{1,0:T(8,128)(2,1)}) %all-gather.19.cloned.1.call-update) | async-done | bytes 6291472 | tf_op jit(solution)/shard_map/all_gather | solution.py:23
  668.7 6.6 fusion.60
  675.4 60.4 %reduce-scatter.19.cloned.1.call-done = f32[1024,192]{0,1:T(8,128)} async-done(((f32[4096,192]{0,1:T(8,128)}), f32[1024,192]{0,1:T(8,128)}) %reduce-scatter.19.cloned.1.call-update) | async-done | bytes 786448 | tf_op jit(solution)/shard_map/reduce_scatter | solution.py:36
  735.8 1.5 multiply_reduce_fusion.1
  737.3 10.1 all-reduce.2
  747.3 2.2 convert_reduce_fusion.4
  749.7 35.4 %all-gather.21.cloned.1.call-done = bf16[4096,192]{0,1:T(8,128)(2,1)} async-done(((bf16[1024,192]{0,1:T(8,128)(2,1)}), bf16[4096,192]{0,1:T(8,128)(2,1)}) %all-gather.21.cloned.1.call-update) | async-done | bytes 1572880 | tf_op jit(solution)/shard_map/all_gather | solution.py:19
  785.0 3.7 fusion.62
  789.8 41.9 %reduce-scatter.21.cloned.1.call-done = f32[1024,192]{0,1:T(8,128)} async-done(((f32[4096,192]{0,1:T(8,128)}), f32[1024,192]{0,1:T(8,128)}) %reduce-scatter.21.cloned.1.call-update) | async-done | bytes 786448 | tf_op jit(solution)/shard_map/reduce_scatter | solution.py:27
  831.7 1.2 convert_element_type.111
  833.0 6.1 multiply_reduce_fusion
  839.1 0.9 slice-done.1
  840.0 1.8 slice-done.2
  841.8 5.2 multiply_convert_fusion
  847.0 4.2 fusion.16
  851.6 2.0 fusion.17
  853.7 2.1 fusion.18
  855.7 1.3 convert_reduce_fusion.1
  857.6 4.9 convolution_convert_fusion.1
  862.4 41.3 %all-gather.15.cloned.1.call-done = bf16[4096,768]{1,0:T(8,128)(2,1)} async-done(((bf16[1024,768]{1,0:T(8,128)(2,1)}), bf16[4096,768]{1,0:T(8,128)(2,1)}) %all-gather.15.cloned.1.call-update) | async-done | bytes 6291472 | tf_op jit(solution)/shard_map/all_gather | solution.py:23
  903.8 5.5 fusion.25
  909.2 1.2 convolution_convert_fusion.2
  910.5 52.1 %all-gather.23.cloned.1.call-done = bf16[4096,3,192]{0,2,1:T(8,128)(2,1)} async-done(((bf16[1024,3,192]{0,2,1:T(8,128)(2,1)}), bf16[4096,3,192]{0,2,1:T(8,128)(2,1)}) %all-gather.23.cloned.1.call-update) | async-done | bytes 4718608 | tf_op jit(solution)/shard_map/all_gather | solution.py:23
  962.6 5.0 fusion.26
  967.9 5.4 convolution_bitcast_fusion
  973.4 0.9 copy-done.16
  974.3 6.8 fusion.58
  983.0 4.3 all-reduce.8.cloned.1.call-done
  987.3 1.8 convert_element_type.122
  989.1 1.8 convert_element_type.126
  990.9 1.9 copy.34
  992.8 1.6 convert_element_type.119
  994.5 56.6 %reduce-scatter.23.cloned.1.call-done = f32[1024,192]{0,1:T(8,128)} async-done(((f32[4096,192]{0,1:T(8,128)}), f32[1024,192]{0,1:T(8,128)}) %reduce-scatter.23.cloned.1.call-update) | async-done | bytes 786448 | tf_op jit(solution)/shard_map/reduce_scatter | solution.py:36
  1051.0 1.5 fusion.44
  1052.5 10.1 all-reduce.1
  1062.7 51.0 %reduce-scatter.15.cloned.1.call-done = f32[1024,192]{0,1:T(8,128)} async-done(((f32[4096,192]{0,1:T(8,128)}), f32[1024,192]{0,1:T(8,128)}) %reduce-scatter.15.cloned.1.call-update) | async-done | bytes 786448 | tf_op jit(solution)/shard_map/reduce_scatter | solution.py:36
  1113.6 2.9 fusion.43
  1117.1 41.7 %all-reduce = (f32[768]{0:T(1024)}, f32[768]{0:T(1024)}, f32[2,768]{1,0:T(2,128)}, f32[768]{0:T(1024)}, f32[768]{0:T(1024)}, /*index=5*/f32[768]{0:T(1024)}, f32[3072]{0:T(1024)}, f32[768]{0:T(1024)}) all-reduce(f32[768]{0:T(1024)S(1)} %dynamic_update_slice.33, ...), channel_id=1, replica_groups=mesh['dp'=2,'row'=4,'col'=4] {'dp','row','col'}, use_global_device_ids=true, to_apply=%region_28.29 | all-reduce | flops 9216 | bytes 73728 | tf_op jit(solution)/shard_map/psum | solution.py:264
  (110 shorter events, 12.4 us)
Async XLA Ops:
  7.2 339.0 %copy-start = (bf16[192,768]{1,0:T(8,128)(2,1)S(1)}, bf16[192,768]{1,0:T(8,128)(2,1)}, u32[]{:S(2)}) copy-start(bf16[192,768]{1,0:T(8,128)(2,1)} %param.25) | copy-start | bytes 884740
  7.2 53.9 %all-gather.9.cloned.1.call-start = ((), (), s32[]{:S(2)}) async-start(), calls=%async_computation.8 | async-start | bytes 1966080 | tf_op jit(solution)/shard_map/all_gather | solution.py:19
  24.4 137.1 %reduce-scatter.9.cloned.1.call-start = ((), (), s32[]{:S(2)}) async-start(), calls=%async_computation.9 | async-start | bytes 11796480 | tf_op jit(solution)/shard_map/reduce_scatter | solution.py:27
  67.5 137.9 %all-gather.11.cloned.1.call-start = ((), (), s32[]{:S(2)}) async-start(), calls=%async_computation.10 | async-start | bytes 1966080 | tf_op jit(solution)/shard_map/all_gather | solution.py:23
  163.5 3.3 copy-start.8
  163.5 5.0 copy-start.11
  166.7 4.6 copy-start.2
  171.3 34.1 %copy-start.17 = (bf16[192,192]{1,0:T(8,128)(2,1)S(1)}, bf16[192,192]{1,0:T(8,128)(2,1)}, u32[]{:S(2)}) copy-start(bf16[192,192]{1,0:T(8,128)(2,1)} %param.21) | copy-start | bytes 221188
  174.3 95.3 %reduce-scatter.11.cloned.1.call-start = ((), (), s32[]{:S(2)}) async-start(), calls=%async_computation.11 | async-start | bytes 3932160 | tf_op jit(solution)/shard_map/reduce_scatter | solution.py:36
  209.2 60.4 %copy-start.4 = (bf16[192,1024]{1,0:T(8,128)(2,1)S(1)}, bf16[192,1024]{1,0:T(8,128)(2,1)}, u32[]{:S(2)}) copy-start(bf16[192,1024]{1,0:T(8,128)(2,1)} %param.15) | copy-start | bytes 1179652
  209.2 99.0 %copy-start.15 = (bf16[192,768]{1,0:T(8,128)(2,1)S(1)}, bf16[192,768]{1,0:T(8,128)(2,1)}, u32[]{:S(2)}) copy-start(bf16[192,768]{1,0:T(8,128)(2,1)} %param.27) | copy-start | bytes 884740
  209.2 99.0 %all-gather.17.cloned.1.call-start = ((), (), s32[]{:S(2)}) async-start(), calls=%async_computation.16 | async-start | bytes 1966080 | tf_op jit(solution)/shard_map/all_gather | solution.py:19
  209.8 136.4 %all-gather.13.cloned.1.call-start = ((), (), s32[]{:S(2)}) async-start(), calls=%async_computation.12 | async-start | bytes 1966080 | tf_op jit(solution)/shard_map/all_gather | solution.py:19
  282.0 186.9 %reduce-scatter.17.cloned.1.call-start = ((), (), s32[]{:S(2)}) async-start(), calls=%async_computation.17 | async-start | bytes 15728640 | tf_op jit(solution)/shard_map/reduce_scatter | solution.py:27
  315.9 276.8 %reduce-scatter.13.cloned.1.call-start = ((), (), s32[]{:S(2)}) async-start(), calls=%async_computation.13 | async-start | bytes 15728640 | tf_op jit(solution)/shard_map/reduce_scatter | solution.py:27
  354.0 314.7 %all-gather.19.cloned.1.call-start = ((), (), s32[]{:S(2)}) async-start(), calls=%async_computation.18 | async-start | bytes 7864320 | tf_op jit(solution)/shard_map/all_gather | solution.py:23
  598.4 137.4 %reduce-scatter.19.cloned.1.call-start = ((), (), s32[]{:S(2)}) async-start(), calls=%async_computation.19 | async-start | bytes 3932160 | tf_op jit(solution)/shard_map/reduce_scatter | solution.py:36
  675.3 72.0 %copy-start.7 = (bf16[192,1024]{1,0:T(8,128)(2,1)S(1)}, bf16[192,1024]{1,0:T(8,128)(2,1)}, u32[]{:S(2)}) copy-start(bf16[192,1024]{1,0:T(8,128)(2,1)} %param.29) | copy-start | bytes 1179652
  675.4 109.6 %all-gather.21.cloned.1.call-start = ((), (), s32[]{:S(2)}) async-start(), calls=%async_computation.20 | async-start | bytes 1966080 | tf_op jit(solution)/shard_map/all_gather | solution.py:19
  749.6 82.1 %reduce-scatter.21.cloned.1.call-start = ((), (), s32[]{:S(2)}) async-start(), calls=%async_computation.21 | async-start | bytes 3932160 | tf_op jit(solution)/shard_map/reduce_scatter | solution.py:27
  788.7 44.2 %copy-start.12 = (bf16[1024,1,192]{0,2,1:T(8,128)(2,1)S(1)}, bf16[1024,1,192]{0,2,1:T(8,128)(2,1)}, u32[]{:S(2)}) copy-start(bf16[1024,1,192]{0,2,1:T(8,128)(2,1)} %copy-done.11) | copy-start | bytes 1179652
  788.8 115.0 %all-gather.15.cloned.1.call-start = ((), (), s32[]{:S(2)}) async-start(), calls=%async_computation.14 | async-start | bytes 7864320 | tf_op jit(solution)/shard_map/all_gather | solution.py:23
  789.5 173.0 %all-gather.23.cloned.1.call-start = ((), (), s32[]{:S(2)}) async-start(), calls=%async_computation.22 | async-start | bytes 5898240 | tf_op jit(solution)/shard_map/all_gather | solution.py:23
  832.9 6.2 slice-start
  832.9 7.1 slice-start.1
  833.0 8.8 slice-start.2
  841.8 5.2 copy-start.9
  847.0 4.6 copy-start.3
  855.7 1.8 copy-start.10
  857.0 130.3 %all-reduce.8.cloned.1.call-start = ((), (), s32[]{:S(2)}) async-start(), calls=%async_computation.24 | async-start | bytes 1966080 | tf_op jit(solution)/shard_map/psum | solution.py:278
  862.4 46.8 %copy-start.6 = (bf16[4096,192]{0,1:T(8,128)(2,1)S(1)}, bf16[4096,192]{0,1:T(8,128)(2,1)}, u32[]{:S(2)}) copy-start(bf16[4096,192]{0,1:T(8,128)(2,1)} %all-gather.11.cloned.1.call-done) | copy-start | bytes 4718596
  903.8 5.5 copy-start.13
  910.5 57.4 %copy-start.14 = (bf16[3,192,192]{2,1,0:T(8,128)(2,1)S(1)}, bf16[3,192,192]{2,1,0:T(8,128)(2,1)}, u32[]{:S(2)}) copy-start(bf16[3,192,192]{2,1,0:T(8,128)(2,1)} %param.19) | copy-start | bytes 663556
  967.5 83.5 %reduce-scatter.23.cloned.1.call-start = ((), (), s32[]{:S(2)}) async-start(), calls=%async_computation.23 | async-start | bytes 3932160 | tf_op jit(solution)/shard_map/reduce_scatter | solution.py:36
  973.3 1.0 copy-start.16
  973.3 140.3 %reduce-scatter.15.cloned.1.call-start = ((), (), s32[]{:S(2)}) async-start(), calls=%async_computation.15 | async-start | bytes 3932160 | tf_op jit(solution)/shard_map/reduce_scatter | solution.py:36
  981.1 132.5 %copy-start.5 = (f32[1024,192]{0,1:T(8,128)S(1)}, f32[1024,192]{0,1:T(8,128)}, u32[]{:S(2)}) copy-start(f32[1024,192]{0,1:T(8,128)} %reduce-scatter.19.cloned.1.call-done) | copy-start | bytes 2359300
  992.8 165.9 %copy-start.1 = (bf16[192,768]{1,0:T(8,128)(2,1)S(1)}, bf16[192,768]{1,0:T(8,128)(2,1)}, u32[]{:S(2)}) copy-start(bf16[192,768]{1,0:T(8,128)(2,1)} %param.25) | copy-start | bytes 884740
Sparse Core Ops, SparseCore 0:
  24.6 36.4 all-gather.8
  67.6 93.8 reduce-scatter.8
  174.4 30.9 all-gather.10
  209.3 60.2 reduce-scatter.10
  271.0 37.1 all-gather.16
  310.2 35.9 all-gather.12
  349.3 119.5 reduce-scatter.16
  472.0 120.7 reduce-scatter.12
  598.5 70.1 all-gather.18
  675.5 60.2 reduce-scatter.18
  749.7 35.2 all-gather.20
  788.9 42.8 reduce-scatter.20
  833.6 70.1 all-gather.14
  905.5 57.0 all-gather.22
  967.7 19.5 all-reduce.7
  989.5 61.4 reduce-scatter.22
  1053.3 60.2 reduce-scatter.14
where the time goes:
time: 1170 us
  waiting for transfers between devices  924 us (79%)
  matrix products  85.4 us (7%)
  blocking collectives  83.4 us (7%)
  other arithmetic  37.2 us (3%)
  local copies, waits for them, and re-layouts  18.6 us (2%)
  between operations  15 us (1%)
    reduce_scatter x4, waiting for transfers between devices, summed_over_row(): lax.psum_scatter(term_fn(jnp.int32(0), row_count * lax.axis_size('row')),...  372 us
    reduce_scatter x4, waiting for transfers between devices, summed_over_col(): lax.psum_scatter(term_fn(jnp.int32(0), row_count * lax.axis_size('col')),...  225 us
    all_gather x4, waiting for transfers between devices, row_rows(): return lax.all_gather(values, 'row', axis=0, tiled=True)  195 us
    all_gather x4, waiting for transfers between devices, column_rows(): return lax.all_gather(values, 'col', axis=0, tiled=True)  127 us
    psum x4, blocking collectives, feature_totals(): return lax.psum(values, 'row')  41.7 us
    psum x1, blocking collectives, on_device(): lax.psum((ln1_gain_part, ln1_bias_part, qv_part, out_bias_part, ln2_gain_...  41.7 us
  transfers between devices with their start and end apart: 17, of which 17 were waited for; matrix products, arithmetic and copies ran while one was open for 7% of the time, Pallas kernels for 0%

commit v1 on v0

--- a/solution.py
+++ b/solution.py
@@ -11,6 +11,22 @@
 masked_score = -1e30
 
 
+def gather_around(x, axis, dim):
+    ways, here, lap = (lax.axis_size(axis), lax.axis_index(axis), x.shape[dim])
+    dims = [n * ways if d == dim else n for d, n in enumerate(x.shape)]
+    full = lax.dynamic_update_slice_in_dim(jnp.zeros(dims, x.dtype), x, here * lap, axis=dim)
+    going_up = going_down = x
+    for far in range(1, ways // 2 + 1):
+        going_up = lax.ppermute(going_up, axis, [(d, (d + 1) % ways) for d in range(ways)])
+        full = lax.dynamic_update_slice_in_dim(full, going_up, (here - far) % ways * lap, axis=dim)
+        if 2 * far < ways:
+            going_down = lax.ppermute(going_down, axis, [(d, (d - 1) % ways) for d in range(ways)])
+            full = lax.dynamic_update_slice_in_dim(
+                full, going_down, (here + far) % ways * lap, axis=dim
+            )
+    return full
+
+
 def feature_totals(values):
     return lax.psum(values, "row")
 
@@ -20,7 +36,7 @@
 
 
 def row_rows(values):
-    return lax.all_gather(values, "row", axis=0, tiled=True)
+    return gather_around(values, "row", 0)
 
 
 def summed_over_row(term_fn, row_count):

time: 1170 us -> 1240 us (1.060)
  waiting for transfers between devices: 924 us -> 968 us
  local copies, waits for them, and re-layouts: 18.6 us -> 35.9 us
  starting transfers between devices: 1.36 us -> 14 us
    ppermute x0 -> x12, waiting for transfers between devices: none -> 282 us  [the longest x8 221 us: gather_around(): lax.ppermute(going_up, axis, [(d, (d + 1) % ways) for d in range(ways)])]
    all_gather x4 -> x0, waiting for transfers between devices: 195 us -> none  [row_rows(): return lax.all_gather(values, 'row', axis=0, tiled=True)]
    reduce_scatter x4, waiting for transfers between devices: 372 us -> 330 us  [summed_over_row(): lax.psum_scatter(term_fn(jnp.int32(0), row_count * lax.axis_size('row')),...]
    ppermute x0 -> x12, starting transfers between devices: none -> 13 us  [the longest x8 7.09 us: gather_around(): lax.ppermute(going_up, axis, [(d, (d + 1) % ways) for d in range(ways)])]
  transfers between devices with their start and end apart: 17 -> 25, of which waited for: 17 -> 25; matrix products, arithmetic and copies ran while one was open for 7% -> 7% of each run, Pallas kernels for 0% -> 0%
where the time goes in v1:
time: 1240 us; the launch traced here: 1230 us
  waiting for transfers between devices  968 us (78%)
  blocking collectives  83.3 us (7%)
  matrix products  74.4 us (6%)
  other arithmetic  39.4 us (3%)
  local copies, waits for them, and re-layouts  35.9 us (3%)
  between operations  15.6 us (1%)
  starting transfers between devices  14 us (1%)
    reduce_scatter x4, waiting for transfers between devices, summed_over_row(): lax.psum_scatter(term_fn(jnp.int32(0), row_count * lax.axis_size('row')),...  330 us
    reduce_scatter x4, waiting for transfers between devices, summed_over_col(): lax.psum_scatter(term_fn(jnp.int32(0), row_count * lax.axis_size('col')),...  225 us
    ppermute x8, waiting for transfers between devices, gather_around(): lax.ppermute(going_up, axis, [(d, (d + 1) % ways) for d in range(ways)])  221 us
    all_gather x4, waiting for transfers between devices, column_rows(): return lax.all_gather(values, 'col', axis=0, tiled=True)  126 us
    ppermute x4, waiting for transfers between devices, gather_around(): lax.ppermute(going_down, axis, [(d, (d - 1) % ways) for d in range(ways)])  61.3 us
    psum x1, blocking collectives, on_device(): lax.psum((ln1_gain_part, ln1_bias_part, qv_part, out_bias_part, ln2_gain_...  41.6 us
    psum x4, blocking collectives, feature_totals(): return lax.psum(values, 'row')  41.6 us
  transfers between devices with their start and end apart: 25, of which 25 were waited for; matrix products, arithmetic and copies ran while one was open for 7% of the time, Pallas kernels for 0%

profile of v1, /device:TPU:0, one launch (start us, length us, event | category | flops | bytes accessed | tf_op | source)
XLA Modules:
  0.0 1230.8 jit_solution(15873586180413765703)
XLA Ops:
  11.0 11.5 all-reduce.4
  22.5 1.9 fusion.38
  25.7 35.4 %all-gather.5.cloned.1.call-done = bf16[4096,192]{0,1:T(8,128)(2,1)} async-done(((bf16[1024,192]{0,1:T(8,128)(2,1)}), bf16[4096,192]{0,1:T(8,128)(2,1)}) %all-gather.5.cloned.1.call-update) | async-done | bytes 1572880 | tf_op jit(solution)/shard_map/all_gather | solution.py:35
  61.1 6.4 fusion.61
  69.6 92.0 %reduce-scatter.9.cloned.1.call-done = f32[1024,3,192]{0,2,1:T(8,128)} async-done(((f32[4096,3,192]{0,2,1:T(8,128)}), f32[1024,3,192]{0,2,1:T(8,128)}) %reduce-scatter.9.cloned.1.call-update) | async-done | bytes 2359312 | tf_op jit(solution)/shard_map/reduce_scatter | solution.py:43
  161.6 1.9 add_convert_fusion
  163.5 3.2 fusion.55
  168.6 2.8 copy-done.2
  171.4 2.3 fusion.21
  176.7 10.0 collective-permute-done
  187.4 7.6 collective-permute-done.1
  195.0 7.3 collective-permute-done.2
  202.4 2.2 fusion.56
  207.6 57.4 %reduce-scatter.11.cloned.1.call-done = f32[1024,192]{0,1:T(8,128)} async-done(((f32[4096,192]{0,1:T(8,128)}), f32[1024,192]{0,1:T(8,128)}) %reduce-scatter.11.cloned.1.call-update) | async-done | bytes 786448 | tf_op jit(solution)/shard_map/reduce_scatter | solution.py:52
  266.3 10.0 all-reduce.3
  277.5 26.1 %all-gather.9.cloned.1.call-done = bf16[4096,192]{0,1:T(8,128)(2,1)} async-done(((bf16[1024,192]{0,1:T(8,128)(2,1)}), bf16[4096,192]{0,1:T(8,128)(2,1)}) %all-gather.9.cloned.1.call-update) | async-done | bytes 1572880 | tf_op jit(solution)/shard_map/all_gather | solution.py:35
  303.6 7.8 fusion.59
  311.9 29.6 %all-gather.7.cloned.1.call-done = bf16[4096,192]{0,1:T(8,128)(2,1)} async-done(((bf16[1024,192]{0,1:T(8,128)(2,1)}), bf16[4096,192]{0,1:T(8,128)(2,1)}) %all-gather.7.cloned.1.call-update) | async-done | bytes 1572880 | tf_op jit(solution)/shard_map/all_gather | solution.py:35
  341.6 7.9 fusion.57
  350.3 113.8 %reduce-scatter.17.cloned.1.call-done = f32[1024,768]{1,0:T(8,128)} async-done(((f32[4096,768]{1,0:T(8,128)}), f32[1024,768]{1,0:T(8,128)}) %reduce-scatter.17.cloned.1.call-update) | async-done | bytes 3145744 | tf_op jit(solution)/shard_map/reduce_scatter | solution.py:43
  464.1 123.9 %reduce-scatter.13.cloned.1.call-done = f32[1024,768]{1,0:T(8,128)} async-done(((f32[4096,768]{1,0:T(8,128)}), f32[1024,768]{1,0:T(8,128)}) %reduce-scatter.13.cloned.1.call-update) | async-done | bytes 3145744 | tf_op jit(solution)/shard_map/reduce_scatter | solution.py:43
  588.0 4.9 convert_reduce_fusion
  595.8 35.3 %collective-permute-done.6 = bf16[1024,768]{1,0:T(8,128)(2,1)S(1)} collective-permute-done((bf16[1024,768]{1,0:T(8,128)(2,1)S(1)}, bf16[1024,768]{1,0:T(8,128)(2,1)S(1)}, u32[]{:S(2)}, u32[]{:S(2)}) %collective-permute-start.6) | collective-permute-done | bytes 1572896 | tf_op jit(solution)/shard_map/ppermute | solution.py:20
  632.2 32.4 %collective-permute-done.7 = bf16[1024,768]{1,0:T(8,128)(2,1)S(1)} collective-permute-done((bf16[1024,768]{1,0:T(8,128)(2,1)S(1)}, bf16[1024,768]{1,0:T(8,128)(2,1)S(1)}, u32[]{:S(2)}, u32[]{:S(2)}) %collective-permute-start.7) | collective-permute-done | bytes 1572896 | tf_op jit(solution)/shard_map/ppermute | solution.py:23
  664.8 32.5 %collective-permute-done.8 = bf16[1024,768]{1,0:T(8,128)(2,1)S(1)} collective-permute-done((bf16[1024,768]{1,0:T(8,128)(2,1)S(1)}, bf16[1024,768]{1,0:T(8,128)(2,1)S(1)}, u32[]{:S(2)}, u32[]{:S(2)}) %collective-permute-start.8) | collective-permute-done | bytes 1572896 | tf_op jit(solution)/shard_map/ppermute | solution.py:20
  697.5 2.6 copy-done.3
  700.1 3.9 fusion.60
  704.1 60.2 %reduce-scatter.19.cloned.1.call-done = f32[1024,192]{0,1:T(8,128)} async-done(((f32[4096,192]{0,1:T(8,128)}), f32[1024,192]{0,1:T(8,128)}) %reduce-scatter.19.cloned.1.call-update) | async-done | bytes 786448 | tf_op jit(solution)/shard_map/reduce_scatter | solution.py:52
  764.3 2.1 multiply_reduce_fusion.1
  766.4 10.0 all-reduce.2
  776.5 2.8 convert_reduce_fusion.4
  779.4 35.3 %all-gather.11.cloned.1.call-done = bf16[4096,192]{0,1:T(8,128)(2,1)} async-done(((bf16[1024,192]{0,1:T(8,128)(2,1)}), bf16[4096,192]{0,1:T(8,128)(2,1)}) %all-gather.11.cloned.1.call-update) | async-done | bytes 1572880 | tf_op jit(solution)/shard_map/all_gather | solution.py:35
  814.7 3.6 fusion.62
  818.4 3.1 broadcast.97.clone.1
  821.6 2.8 constant_dynamic-update-slice_fusion.11
  827.3 59.1 %collective-permute-done.3 = bf16[1024,768]{1,0:T(8,128)(2,1)} collective-permute-done((bf16[1024,768]{1,0:T(8,128)(2,1)}, bf16[1024,768]{1,0:T(8,128)(2,1)}, u32[]{:S(2)}, u32[]{:S(2)}) %collective-permute-start.3) | collective-permute-done | bytes 1572896 | tf_op jit(solution)/shard_map/ppermute | solution.py:20
  888.1 6.2 multiply_reduce_fusion
  896.5 5.3 multiply_convert_fusion
  901.8 4.1 fusion.16
  905.9 2.1 fusion.18
  908.1 2.0 fusion.17
  912.0 2.9 constant_dynamic-update-slice_fusion.10
  914.9 4.3 collective-permute-done.4
  919.1 2.7 constant_dynamic-update-slice_fusion.9
  921.8 2.2 convolution_convert_fusion.1
  925.2 28.7 %collective-permute-done.5 = bf16[1024,768]{1,0:T(8,128)(2,1)} collective-permute-done((bf16[1024,768]{1,0:T(8,128)(2,1)}, bf16[1024,768]{1,0:T(8,128)(2,1)}, u32[]{:S(2)}, u32[]{:S(2)}) %collective-permute-start.5) | collective-permute-done | bytes 1572896 | tf_op jit(solution)/shard_map/ppermute | solution.py:20
  953.8 2.7 constant_dynamic-update-slice_fusion.8
  956.5 22.5 %collective-permute-done.9 = bf16[1024,3,192]{0,2,1:T(8,128)(2,1)S(1)} collective-permute-done((bf16[1024,3,192]{0,2,1:T(8,128)(2,1)S(1)}, bf16[1024,3,192]{0,2,1:T(8,128)(2,1)S(1)}, u32[]{:S(2)}, u32[]{:S(2)}) %collective-permute-start.9) | collective-permute-done | bytes 1179680 | tf_op jit(solution)/shard_map/ppermute | solution.py:20
  979.2 4.9 fusion.25
  986.3 17.0 %collective-permute-done.10 = bf16[1024,3,192]{0,2,1:T(8,128)(2,1)S(1)} collective-permute-done((bf16[1024,3,192]{0,2,1:T(8,128)(2,1)S(1)}, bf16[1024,3,192]{0,2,1:T(8,128)(2,1)S(1)}, u32[]{:S(2)}, u32[]{:S(2)}) %collective-permute-start.10) | collective-permute-done | bytes 1179680 | tf_op jit(solution)/shard_map/ppermute | solution.py:23
  1003.4 25.6 %collective-permute-done.11 = bf16[1024,3,192]{0,2,1:T(8,128)(2,1)S(1)} collective-permute-done((bf16[1024,3,192]{0,2,1:T(8,128)(2,1)S(1)}, bf16[1024,3,192]{0,2,1:T(8,128)(2,1)S(1)}, u32[]{:S(2)}, u32[]{:S(2)}) %collective-permute-start.11) | collective-permute-done | bytes 1179680 | tf_op jit(solution)/shard_map/ppermute | solution.py:20
  1029.2 2.1 copy-done.4
  1031.3 2.1 fusion.26
  1033.5 5.4 convolution_bitcast_fusion
  1039.9 6.7 fusion.58
  1048.8 3.5 all-reduce.8.cloned.1.call-done
  1052.3 1.8 convert_element_type.121
  1054.1 1.8 convert_element_type.125
  1055.9 1.9 copy.34
  1059.5 56.6 %reduce-scatter.23.cloned.1.call-done = f32[1024,192]{0,1:T(8,128)} async-done(((f32[4096,192]{0,1:T(8,128)}), f32[1024,192]{0,1:T(8,128)}) %reduce-scatter.23.cloned.1.call-update) | async-done | bytes 786448 | tf_op jit(solution)/shard_map/reduce_scatter | solution.py:52
  1117.6 10.1 all-reduce.1
  1127.7 51.2 %reduce-scatter.15.cloned.1.call-done = f32[1024,192]{0,1:T(8,128)} async-done(((f32[4096,192]{0,1:T(8,128)}), f32[1024,192]{0,1:T(8,128)}) %reduce-scatter.15.cloned.1.call-update) | async-done | bytes 786448 | tf_op jit(solution)/shard_map/reduce_scatter | solution.py:52
  1178.9 2.9 fusion.43
  1182.4 41.6 %all-reduce = (f32[768]{0:T(1024)}, f32[768]{0:T(1024)}, f32[2,768]{1,0:T(2,128)}, f32[768]{0:T(1024)}, f32[768]{0:T(1024)}, /*index=5*/f32[768]{0:T(1024)}, f32[3072]{0:T(1024)}, f32[768]{0:T(1024)}) all-reduce(f32[768]{0:T(1024)S(1)} %dynamic_update_slice.97, ...), channel_id=1, replica_groups=mesh['dp'=2,'row'=4,'col'=4] {'dp','row','col'}, use_global_device_ids=true, to_apply=%region_28.29 | all-reduce | flops 9216 | bytes 73728 | tf_op jit(solution)/shard_map/psum | solution.py:280
  (216 shorter events, 42.5 us)
Async XLA Ops:
  7.2 334.4 %copy-start = (bf16[192,768]{1,0:T(8,128)(2,1)S(1)}, bf16[192,768]{1,0:T(8,128)(2,1)}, u32[]{:S(2)}) copy-start(bf16[192,768]{1,0:T(8,128)(2,1)} %param.25) | copy-start | bytes 884740
  7.2 53.9 %all-gather.5.cloned.1.call-start = ((), (), s32[]{:S(2)}) async-start(), calls=%async_computation.8 | async-start | bytes 1966080 | tf_op jit(solution)/shard_map/all_gather | solution.py:35
  10.2 14.3 %copy-start.45 = (f32[192]{0:T(256)}, f32[192]{0:T(256)S(1)}, u32[]{:S(2)}) copy-start(f32[192]{0:T(256)S(1)} %dynamic_slice.40) | copy-start | bytes 2308
  24.5 137.1 %reduce-scatter.9.cloned.1.call-start = ((), (), s32[]{:S(2)}) async-start(), calls=%async_computation.9 | async-start | bytes 11796480 | tf_op jit(solution)/shard_map/reduce_scatter | solution.py:43
  67.6 197.4 %reduce-scatter.11.cloned.1.call-start = ((), (), s32[]{:S(2)}) async-start(), calls=%async_computation.10 | async-start | bytes 3932160 | tf_op jit(solution)/shard_map/reduce_scatter | solution.py:52
  163.5 5.1 copy-start.16
  168.6 5.1 copy-start.29
  173.7 28.7 %copy-start.22 = (bf16[192,192]{1,0:T(8,128)(2,1)S(1)}, bf16[192,192]{1,0:T(8,128)(2,1)}, u32[]{:S(2)}) copy-start(bf16[192,192]{1,0:T(8,128)(2,1)} %param.21) | copy-start | bytes 221188
  173.7 13.0 %collective-permute-start = (bf16[1024,192]{0,1:T(8,128)(2,1)S(1)}, bf16[1024,192]{0,1:T(8,128)(2,1)S(1)}, u32[]{:S(2)}, u32[]{:S(2)}) collective-permute-start(bf16[1024,192]{0,1:T(8,128)(2,1)S(1)} %bitcast.140), channel_id=1, source_target_pairs={{0,4},{4,8},{8,12},{12,0},{1,5},{5,9},{9,13},{13,1},{2,6},{6,10},{... | collective-permute-start | bytes 1179656 | tf_op jit(solution)/shard_map/ppermute | solution.py:20
  175.1 19.9 %collective-permute-start.1 = (bf16[1024,192]{0,1:T(8,128)(2,1)S(1)}, bf16[1024,192]{0,1:T(8,128)(2,1)S(1)}, u32[]{:S(2)}, u32[]{:S(2)}) collective-permute-start(bf16[1024,192]{0,1:T(8,128)(2,1)S(1)} %bitcast.141), channel_id=1, source_target_pairs={{0,12},{4,0},{8,4},{12,8},{1,13},{5,1},{9,5},{13,9},{2,14},{6,2},{... | collective-permute-start | bytes 1179656 | tf_op jit(solution)/shard_map/ppermute | solution.py:23
  186.7 15.7 %collective-permute-start.2 = (bf16[1024,192]{0,1:T(8,128)(2,1)S(1)}, bf16[1024,192]{0,1:T(8,128)(2,1)S(1)}, u32[]{:S(2)}, u32[]{:S(2)}) collective-permute-start(bf16[1024,192]{0,1:T(8,128)(2,1)S(1)} %collective-permute-done), channel_id=1, source_target_pairs={{0,4},{4,8},{8,12},{12,0},{1,5},{5,9},{9,13},{13,1},{2,6},{6,10},{... | collective-permute-start | bytes 1179656 | tf_op jit(solution)/shard_map/ppermute | solution.py:20
  204.7 60.4 %copy-start.5 = (bf16[192,1024]{1,0:T(8,128)(2,1)S(1)}, bf16[192,1024]{1,0:T(8,128)(2,1)}, u32[]{:S(2)}) copy-start(bf16[192,1024]{1,0:T(8,128)(2,1)} %param.15) | copy-start | bytes 1179652
  204.7 98.9 %copy-start.20 = (bf16[192,768]{1,0:T(8,128)(2,1)S(1)}, bf16[192,768]{1,0:T(8,128)(2,1)}, u32[]{:S(2)}) copy-start(bf16[192,768]{1,0:T(8,128)(2,1)} %param.27) | copy-start | bytes 884740
  204.7 98.9 %all-gather.9.cloned.1.call-start = ((), (), s32[]{:S(2)}) async-start(), calls=%async_computation.14 | async-start | bytes 1966080 | tf_op jit(solution)/shard_map/all_gather | solution.py:35
  205.3 136.3 %all-gather.7.cloned.1.call-start = ((), (), s32[]{:S(2)}) async-start(), calls=%async_computation.11 | async-start | bytes 1966080 | tf_op jit(solution)/shard_map/all_gather | solution.py:35
  206.8 104.6 %copy-start.41 = (f32[192]{0:T(256)}, f32[192]{0:T(256)S(1)}, u32[]{:S(2)}) copy-start(f32[192]{0:T(256)S(1)} %dynamic_slice.44) | copy-start | bytes 2308
  276.4 35.0 %copy-start.23 = (f32[1024]{0:T(1024)}, f32[1024]{0:T(1024)S(1)}, u32[]{:S(2)}) copy-start(f32[1024]{0:T(1024)S(1)} %get-tuple-element.110) | copy-start | bytes 12292
  276.4 35.0 %copy-start.26 = (f32[1024]{0:T(1024)}, f32[1024]{0:T(1024)S(1)}, u32[]{:S(2)}) copy-start(f32[1024]{0:T(1024)S(1)} %get-tuple-element.111) | copy-start | bytes 12292
  277.4 186.7 %reduce-scatter.17.cloned.1.call-start = ((), (), s32[]{:S(2)}) async-start(), calls=%async_computation.15 | async-start | bytes 15728640 | tf_op jit(solution)/shard_map/reduce_scatter | solution.py:43
  311.4 276.6 %reduce-scatter.13.cloned.1.call-start = ((), (), s32[]{:S(2)}) async-start(), calls=%async_computation.12 | async-start | bytes 15728640 | tf_op jit(solution)/shard_map/reduce_scatter | solution.py:43
  349.4 414.9 %reduce-scatter.19.cloned.1.call-start = ((), (), s32[]{:S(2)}) async-start(), calls=%async_computation.16 | async-start | bytes 3932160 | tf_op jit(solution)/shard_map/reduce_scatter | solution.py:52
  350.3 242.6 %copy-start.35 = (f32[768]{0:T(1024)}, f32[768]{0:T(1024)S(1)}, u32[]{:S(2)}) copy-start(f32[768]{0:T(1024)S(1)} %dynamic_slice.46) | copy-start | bytes 9220
  592.9 38.2 %collective-permute-start.6 = (bf16[1024,768]{1,0:T(8,128)(2,1)S(1)}, bf16[1024,768]{1,0:T(8,128)(2,1)S(1)}, u32[]{:S(2)}, u32[]{:S(2)}) collective-permute-start(bf16[1024,768]{1,0:T(8,128)(2,1)S(1)} %get-tuple-element.92), channel_id=1, source_target_pairs={{0,4},{4,8},{8,12},{12,0},{1,5},{5,9},{9,13},{13,1},{2,6},{6,10},{... | collective-permute-start | bytes 4718600 | tf_op jit(solution)/shard_map/ppermute | solution.py:20
  594.2 70.5 %collective-permute-start.7 = (bf16[1024,768]{1,0:T(8,128)(2,1)S(1)}, bf16[1024,768]{1,0:T(8,128)(2,1)S(1)}, u32[]{:S(2)}, u32[]{:S(2)}) collective-permute-start(bf16[1024,768]{1,0:T(8,128)(2,1)S(1)} %get-tuple-element.92), channel_id=1, source_target_pairs={{0,12},{4,0},{8,4},{12,8},{1,13},{5,1},{9,5},{13,9},{2,14},{6,2},{... | collective-permute-start | bytes 4718600 | tf_op jit(solution)/shard_map/ppermute | solution.py:23
  631.0 66.3 %collective-permute-start.8 = (bf16[1024,768]{1,0:T(8,128)(2,1)S(1)}, bf16[1024,768]{1,0:T(8,128)(2,1)S(1)}, u32[]{:S(2)}, u32[]{:S(2)}) collective-permute-start(bf16[1024,768]{1,0:T(8,128)(2,1)S(1)} %collective-permute-done.6), channel_id=1, source_target_pairs={{0,4},{4,8},{8,12},{12,0},{1,5},{5,9},{9,13},{13,1},{2,6},{6,10},{... | collective-permute-start | bytes 4718600 | tf_op jit(solution)/shard_map/ppermute | solution.py:20
  704.0 60.3 %copy-start.24 = (f32[1024]{0:T(1024)S(1)}, f32[1024]{0:T(1024)}, u32[]{:S(2)}) copy-start(f32[1024]{0:T(1024)} %copy-done.23) | copy-start | bytes 12292
  704.0 60.3 %copy-start.27 = (f32[1024]{0:T(1024)S(1)}, f32[1024]{0:T(1024)}, u32[]{:S(2)}) copy-start(f32[1024]{0:T(1024)} %copy-done.26) | copy-start | bytes 12292
  704.0 60.3 %copy-start.42 = (f32[192]{0:T(256)S(1)}, f32[192]{0:T(256)}, u32[]{:S(2)}) copy-start(f32[192]{0:T(256)} %copy-done.41) | copy-start | bytes 2308
  704.0 72.5 %copy-start.8 = (bf16[192,1024]{1,0:T(8,128)(2,1)S(1)}, bf16[192,1024]{1,0:T(8,128)(2,1)}, u32[]{:S(2)}) copy-start(bf16[192,1024]{1,0:T(8,128)(2,1)} %param.29) | copy-start | bytes 1179652
  704.0 110.7 %all-gather.11.cloned.1.call-start = ((), (), s32[]{:S(2)}) async-start(), calls=%async_computation.17 | async-start | bytes 1966080 | tf_op jit(solution)/shard_map/all_gather | solution.py:35
  776.5 41.9 %copy-start.37 = (f32[1024]{0:T(1024)}, f32[1024]{0:T(1024)S(1)}, u32[]{:S(2)}) copy-start(f32[1024]{0:T(1024)S(1)} %get-tuple-element.118) | copy-start | bytes 12292
  776.5 41.8 %copy-start.39 = (f32[1024]{0:T(1024)}, f32[1024]{0:T(1024)S(1)}, u32[]{:S(2)}) copy-start(f32[1024]{0:T(1024)S(1)} %get-tuple-element.119) | copy-start | bytes 12292
  779.3 107.6 %reduce-scatter.21.cloned.1.call-start = ((), (), s32[]{:S(2)}) async-start(), calls=%async_computation.18 | async-start | bytes 3932160 | tf_op jit(solution)/shard_map/reduce_scatter | solution.py:43
  818.4 233.9 %all-reduce.8.cloned.1.call-start = ((), (), s32[]{:S(2)}) async-start(), calls=%async_computation.20 | async-start | bytes 1966080 | tf_op jit(solution)/shard_map/psum | solution.py:294
  824.4 62.1 %collective-permute-start.3 = (bf16[1024,768]{1,0:T(8,128)(2,1)}, bf16[1024,768]{1,0:T(8,128)(2,1)}, u32[]{:S(2)}, u32[]{:S(2)}) collective-permute-start(bf16[1024,768]{1,0:T(8,128)(2,1)} %get-tuple-element.98), channel_id=1, source_target_pairs={{0,4},{4,8},{8,12},{12,0},{1,5},{5,9},{9,13},{13,1},{2,6},{6,10},{... | collective-permute-start | bytes 4718600 | tf_op jit(solution)/shard_map/ppermute | solution.py:20
  825.9 93.3 %collective-permute-start.4 = (bf16[1024,768]{1,0:T(8,128)(2,1)}, bf16[1024,768]{1,0:T(8,128)(2,1)}, u32[]{:S(2)}, u32[]{:S(2)}) collective-permute-start(bf16[1024,768]{1,0:T(8,128)(2,1)} %get-tuple-element.98), channel_id=1, source_target_pairs={{0,12},{4,0},{8,4},{12,8},{1,13},{5,1},{9,5},{13,9},{2,14},{6,2},{... | collective-permute-start | bytes 4718600 | tf_op jit(solution)/shard_map/ppermute | solution.py:23
  886.4 67.4 %collective-permute-start.5 = (bf16[1024,768]{1,0:T(8,128)(2,1)}, bf16[1024,768]{1,0:T(8,128)(2,1)}, u32[]{:S(2)}, u32[]{:S(2)}) collective-permute-start(bf16[1024,768]{1,0:T(8,128)(2,1)} %collective-permute-done.3), channel_id=1, source_target_pairs={{0,4},{4,8},{8,12},{12,0},{1,5},{5,9},{9,13},{13,1},{2,6},{6,10},{... | collective-permute-start | bytes 4718600 | tf_op jit(solution)/shard_map/ppermute | solution.py:20
  888.1 6.3 slice-start
  888.1 7.2 slice-start.1
  888.1 8.4 slice-start.2
  896.5 5.3 copy-start.13
  901.8 6.2 slice-start.3
  908.0 13.8 %slice-start.5 = ((s8[6291456]{0:T(1024)(128)(4,1)}), s8[2097152]{0:T(1024)(128)(4,1)S(1)}, s32[]{:S(2)}) async-start(s8[6291456]{0:T(1024)(128)(4,1)} %bitcast.125), calls=%async_computation.26 | async-start | bytes 4194304
  910.1 11.7 slice-start.6
  910.3 68.7 %collective-permute-start.9 = (bf16[1024,3,192]{0,2,1:T(8,128)(2,1)S(1)}, bf16[1024,3,192]{0,2,1:T(8,128)(2,1)S(1)}, u32[]{:S(2)}, u32[]{:S(2)}) collective-permute-start(bf16[1024,3,192]{0,2,1:T(8,128)(2,1)S(1)} %get-tuple-element.96), channel_id=1, source_target_pairs={{0,4},{4,8},{8,12},{12,0},{1,5},{5,9},{9,13},{13,1},{2,6},{6,10},{... | collective-permute-start | bytes 3538952 | tf_op jit(solution)/shard_map/ppermute | solution.py:20
  912.0 9.8 copy-start.15
  924.0 55.2 %copy-start.14 = (bf16[4096,192]{0,1:T(8,128)(2,1)S(1)}, bf16[4096,192]{0,1:T(8,128)(2,1)}, u32[]{:S(2)}) copy-start(bf16[4096,192]{0,1:T(8,128)(2,1)} %all-gather.9.cloned.1.call-done) | copy-start | bytes 4718596
  924.0 79.3 %collective-permute-start.10 = (bf16[1024,3,192]{0,2,1:T(8,128)(2,1)S(1)}, bf16[1024,3,192]{0,2,1:T(8,128)(2,1)S(1)}, u32[]{:S(2)}, u32[]{:S(2)}) collective-permute-start(bf16[1024,3,192]{0,2,1:T(8,128)(2,1)S(1)} %get-tuple-element.96), channel_id=1, source_target_pairs={{0,12},{4,0},{8,4},{12,8},{1,13},{5,1},{9,5},{13,9},{2,14},{6,2},{... | collective-permute-start | bytes 3538952 | tf_op jit(solution)/shard_map/ppermute | solution.py:23
  956.5 27.6 %copy-start.18 = (bf16[4096,192]{0,1:T(8,128)(2,1)S(1)}, bf16[4096,192]{0,1:T(8,128)(2,1)}, u32[]{:S(2)}) copy-start(bf16[4096,192]{0,1:T(8,128)(2,1)} %all-gather.11.cloned.1.call-done) | copy-start | bytes 4718596
  979.0 50.0 %collective-permute-start.11 = (bf16[1024,3,192]{0,2,1:T(8,128)(2,1)S(1)}, bf16[1024,3,192]{0,2,1:T(8,128)(2,1)S(1)}, u32[]{:S(2)}, u32[]{:S(2)}) collective-permute-start(bf16[1024,3,192]{0,2,1:T(8,128)(2,1)S(1)} %collective-permute-done.9), channel_id=1, source_target_pairs={{0,4},{4,8},{8,12},{12,0},{1,5},{5,9},{9,13},{13,1},{2,6},{6,10},{... | collective-permute-start | bytes 3538952 | tf_op jit(solution)/shard_map/ppermute | solution.py:20
  986.1 45.2 %copy-start.17 = (bf16[4096,192]{0,1:T(8,128)(2,1)S(1)}, bf16[4096,192]{0,1:T(8,128)(2,1)}, u32[]{:S(2)}) copy-start(bf16[4096,192]{0,1:T(8,128)(2,1)} %all-gather.5.cloned.1.call-done) | copy-start | bytes 4718596
  1033.5 82.6 %reduce-scatter.23.cloned.1.call-start = ((), (), s32[]{:S(2)}) async-start(), calls=%async_computation.19 | async-start | bytes 3932160 | tf_op jit(solution)/shard_map/reduce_scatter | solution.py:52
  1039.0 139.8 %reduce-scatter.15.cloned.1.call-start = ((), (), s32[]{:S(2)}) async-start(), calls=%async_computation.13 | async-start | bytes 3932160 | tf_op jit(solution)/shard_map/reduce_scatter | solution.py:52
  1046.7 69.4 %copy-start.32 = (f32[1024]{0:T(1024)S(1)}, f32[1024]{0:T(1024)}, u32[]{:S(2)}) copy-start(f32[1024]{0:T(1024)} %copy-done.31) | copy-start | bytes 12292
  1046.7 69.4 %copy-start.34 = (f32[1024]{0:T(1024)S(1)}, f32[1024]{0:T(1024)}, u32[]{:S(2)}) copy-start(f32[1024]{0:T(1024)} %copy-done.33) | copy-start | bytes 12292
  1046.7 69.4 %copy-start.46 = (f32[192]{0:T(256)S(1)}, f32[192]{0:T(256)}, u32[]{:S(2)}) copy-start(f32[192]{0:T(256)} %copy-done.45) | copy-start | bytes 2308
  1046.7 132.1 %copy-start.7 = (f32[1024,192]{0,1:T(8,128)S(1)}, f32[1024,192]{0,1:T(8,128)}, u32[]{:S(2)}) copy-start(f32[1024,192]{0,1:T(8,128)} %reduce-scatter.19.cloned.1.call-done) | copy-start | bytes 2359300
  1046.7 132.1 %copy-start.9 = (bf16[192,1024]{1,0:T(8,128)(2,1)S(1)}, bf16[192,1024]{1,0:T(8,128)(2,1)}, u32[]{:S(2)}) copy-start(bf16[192,1024]{1,0:T(8,128)(2,1)} %param.29) | copy-start | bytes 1179652
  1046.7 132.1 %copy-start.25 = (f32[1024]{0:T(1024)S(1)}, f32[1024]{0:T(1024)}, u32[]{:S(2)}) copy-start(f32[1024]{0:T(1024)} %copy-done.23) | copy-start | bytes 12292
  1046.7 132.1 %copy-start.28 = (f32[1024]{0:T(1024)S(1)}, f32[1024]{0:T(1024)}, u32[]{:S(2)}) copy-start(f32[1024]{0:T(1024)} %copy-done.26) | copy-start | bytes 12292
  1046.7 132.1 %copy-start.38 = (f32[1024]{0:T(1024)S(1)}, f32[1024]{0:T(1024)}, u32[]{:S(2)}) copy-start(f32[1024]{0:T(1024)} %copy-done.37) | copy-start | bytes 12292
  1046.7 132.1 %copy-start.40 = (f32[1024]{0:T(1024)S(1)}, f32[1024]{0:T(1024)}, u32[]{:S(2)}) copy-start(f32[1024]{0:T(1024)} %copy-done.39) | copy-start | bytes 12292
  1046.8 132.1 %copy-start.43 = (f32[192]{0:T(256)S(1)}, f32[192]{0:T(256)}, u32[]{:S(2)}) copy-start(f32[192]{0:T(256)} %copy-done.41) | copy-start | bytes 2308
  1057.9 166.2 %copy-start.1 = (bf16[192,768]{1,0:T(8,128)(2,1)S(1)}, bf16[192,768]{1,0:T(8,128)(2,1)}, u32[]{:S(2)}) copy-start(bf16[192,768]{1,0:T(8,128)(2,1)} %param.25) | copy-start | bytes 884740
  (18 other events, 43.4 us)
Sparse Core Ops, SparseCore 0:
  24.6 36.4 all-gather.4
  67.7 93.8 reduce-scatter.8
  204.8 60.1 reduce-scatter.10
  266.4 37.1 all-gather.8
  305.6 35.9 all-gather.6
  344.5 119.5 reduce-scatter.16
  467.2 120.7 reduce-scatter.12
  704.2 60.1 reduce-scatter.18
  779.5 35.2 all-gather.10
  818.5 68.3 reduce-scatter.20
  1033.6 18.6 all-reduce.7
  1054.6 61.4 reduce-scatter.22
  1118.5 60.2 reduce-scatter.14
